TPU v7x, 512 devices: a whole 4x4x16 slice. The times are simulated.
512 devices in a mesh: grp: 16 (over y_lo, x, core), mem: 32 (over y_hi, z).
Axes of the slice: x: 4, y: 4 (y_hi: 2, y_lo: 2; y = y_hi * 2 + y_lo), z: 16, core: 2. Of those that a mesh axis runs over, the one named last changes fastest.
Arguments:
- features: float32 [12288, 256], P('mem'), may hold values from -6 to 6
- patterns: bfloat16 [16, 32, 32, 2, 128, 128], P('grp', 'mem'), may hold values from 0 to 2, as said below
- src_tile: int32 [16, 32, 32, 2], P('grp', 'mem'), may hold values from 0 to 2
- dst_tile: int32 [16, 32, 32, 2], P('grp', 'mem'), may hold values from 0 to 2
- tile_count: int32 [16, 32], P('grp', 'mem'), may hold values from 16 to 64, as said below
- cotangent: float32 [12288, 256], P(('mem', 'grp')), may hold values from -6 to 6
- w_self: float32 [256, 256], replicated, may hold values from -0.375 to 0.375
- w_neigh: float32 [256, 256], replicated, may hold values from -0.375 to 0.375
- bias: float32 [256], replicated, may hold values from -3 to 3
Outputs:
- layer_out: float32 [12288, 256], P(('mem', 'grp'))
- grad_self: float32 [256, 256], replicated
- grad_neigh: float32 [256, 256], replicated
- grad_bias: float32 [256], replicated
Inputs may be any that keep to these rules, and one draw needn't show every extreme that they name: `tile_count`: some group has all 64 slots live for some destination block. `patterns`: edge weights are zero or positive.
All inputs are finite; a program needn't handle non-finite values.
Results may differ from a plain program's by a relative error of at most 0.0003.
Values sent between devices are 32-bit elements; how exact they have to be, the bound alone decides.
A program may use at most 64 MiB of HBM per device.

v0:
```python
import jax
import jax.numpy as jnp
from jax import lax
from jax.sharding import PartitionSpec as P


def accumulate(masks, place, rows):
    contrib = jnp.einsum("jpab,jpbd->jpad", masks, rows, precision=lax.Precision.HIGHEST)
    return jnp.einsum("jpt,jpad->tad", place, contrib, precision=lax.Precision.HIGHEST)


def finish(summed, degree, own, cotangent, w_self, w_neigh, bias):
    neigh = summed / jnp.sqrt(1.0 + degree)[:, None]
    pre = jnp.dot(own, w_self, precision=lax.Precision.HIGHEST, preferred_element_type=jnp.float32)
    pre = (
        pre
        + jnp.dot(
            neigh, w_neigh, precision=lax.Precision.HIGHEST, preferred_element_type=jnp.float32
        )
        + bias
    )
    sig = jax.nn.sigmoid(pre)
    layer_out = pre * sig
    dpre = cotangent * sig * (1.0 + pre * (1.0 - sig))
    grad_self = jnp.dot(
        own.T, dpre, precision=lax.Precision.HIGHEST, preferred_element_type=jnp.float32
    )
    grad_neigh = jnp.dot(
        neigh.T, dpre, precision=lax.Precision.HIGHEST, preferred_element_type=jnp.float32
    )
    return (layer_out, grad_self, grad_neigh, jnp.sum(dpre, axis=0))


def on_device(features, patterns, src_tile, dst_tile, tile_count, cotangent, w_self, w_neigh, bias):
    weights = patterns[0, 0]
    sources = src_tile[0, 0]
    targets = dst_tile[0, 0]
    tile = weights.shape[2]
    members = weights.shape[0]
    slots = weights.shape[1]
    block = features.shape[0]
    width = features.shape[1]
    tblocks = block // tile
    order = jnp.arange(members)[:, None] * slots + jnp.arange(slots)[None, :]
    live = (order < tile_count[0, 0]).astype(jnp.float32)
    place = (targets[..., None] == jnp.arange(tblocks)).astype(jnp.float32) * live[..., None]
    masks = weights.astype(jnp.float32)
    degree = jnp.einsum(
        "jpt,jpa->ta", place, jnp.sum(masks, axis=3), precision=lax.Precision.HIGHEST
    ).reshape(block)
    piece = lax.all_gather(features, "mem", axis=0, tiled=True)
    shards = piece.shape[0] // block
    stacked = piece.reshape(shards * tblocks, tile, width)
    picked = jnp.arange(shards)[:, None] * tblocks + sources
    summed = accumulate(masks, place, stacked[picked])
    summed = summed.reshape(block, width)
    share = cotangent.shape[0]
    offset = lax.axis_index("grp") * share
    own = lax.dynamic_slice_in_dim(features, offset, share, 0)
    part_sum, part_degree = (
        lax.psum_scatter(summed, "grp", scatter_dimension=0, tiled=True),
        lax.psum_scatter(degree, "grp", scatter_dimension=0, tiled=True),
    )
    layer_out, grad_self, grad_neigh, grad_bias = finish(
        part_sum, part_degree, own, cotangent, w_self, w_neigh, bias
    )
    grad_self, grad_neigh, grad_bias = lax.psum((grad_self, grad_neigh, grad_bias), ("grp", "mem"))
    return (layer_out, grad_self, grad_neigh, grad_bias)


def solution(mesh):
    placed = (
        P("mem", None),
        P("grp", "mem", None, None, None, None),
        P("grp", "mem", None, None),
        P("grp", "mem", None, None),
        P("grp", "mem"),
        P(("mem", "grp"), None),
        P(),
        P(),
        P(),
    )
    return jax.shard_map(
        on_device,
        mesh=mesh,
        in_specs=placed,
        out_specs=(P(("mem", "grp"), None), P(), P(), P()),
        check_vma=False,
    )
```

profile of v0, /device:TPU:1, one launch (start us, length us, event | category | flops | bytes accessed | tf_op | source)
XLA Modules:
  0.0 824.0 jit_solution(17553899040861458311)
XLA Ops:
  7.2 0.7 all-gather.2.cloned.1.call-update
  8.6 0.7 compare_select_fusion
  9.3 0.1 copy.16
  9.4 0.1 reshape.97
  9.5 227.4 %all-gather.2.cloned.1.call-done = f32[12288,256]{1,0:T(8,128)} async-done(((f32[384,256]{1,0:T(8,128)}), f32[12288,256]{1,0:T(8,128)}) %all-gather.2.cloned.1.call-update) | async-done | bytes 12582928 | tf_op jit(solution)/shard_map/all_gather | solution.py:51
  236.9 9.0 %gather_fusion = f32[64,128,256]{2,1,0:T(8,128)} fusion(f32[96,128,256]{2,1,0:T(8,128)} %bitcast.37, s32[1024]{0:T(1024)S(1)} %pad_clamp_fusion), kind=kCustom, calls=%fused_computation | custom fusion | bytes 16777472 | tf_op jit(solution)/shard_map/gather | solution.py:55
  246.0 11.7 %convolution_bitcast_fusion = f32[32,2,128,256]{2,3,1,0:T(8,128)} fusion(f32[32,2,128,256]{3,2,1,0:T(8,128)} %bitcast.36, bf16[1,1,32,2,128,128]{5,4,3,2,1,0:T(8,128)(2,1)S(1)} %copy-done.1), kind=kOutput, calls=%fused_computation.2 | convolution fusion | flops 3221225472 | bytes 18874368 | tf_op jit(solution)/shard_map/jpab,jpbd->jpad/dot_general | solution.py:8
  257.7 10.4 %copy.18 = f32[32,2,128,256]{3,0,1,2:T(8,128)} copy(f32[32,2,128,256]{2,3,1,0:T(8,128)} %convolution_bitcast_fusion) | data formatting | bytes 16777216 | tf_op jit(solution)/shard_map/jpab,jpbd->jpad/dot_general | solution.py:8
  268.0 6.6 convolution_bitcast_fusion.1
  274.6 0.8 copy.19
  275.5 1.3 dynamic-slice
  277.4 0.6 convert_reduce_fusion
  278.1 0.2 convolution_bitcast_fusion.2
  278.3 31.2 %all-reduce = f32[384]{0:T(512)S(1)} all-reduce(f32[384]{0:T(512)S(1)} %convolution_bitcast_fusion.2), channel_id=3, replica_groups=mesh['grp'=16,'mem'=32] {'grp'}, use_global_device_ids=true, to_apply=%region_2.0.clone | all-reduce | flops 384 | bytes 3072
  309.5 0.1 fusion.16
  309.6 1.0 fusion.6
  310.5 30.5 %reduce-scatter.2.cloned.1.call-done = f32[24,256]{1,0:T(8,128)} async-done(((f32[384,256]{1,0:T(8,128)}), f32[24,256]{1,0:T(8,128)}) %reduce-scatter.2.cloned.1.call-update) | async-done | bytes 24592 | tf_op jit(solution)/shard_map/reduce_scatter | solution.py:61
  341.0 1.6 fusion.21
  342.7 1.9 fusion.4
  344.5 1.9 fusion.9
  346.5 106.5 %psum.23 = f32[256]{0:T(256)} all-reduce(f32[256]{0:T(256)S(1)} %get-tuple-element.6), channel_id=1, replica_groups=mesh['grp'=16,'mem'=32] {'grp','mem'}, use_global_device_ids=true, to_apply=%region_6.0 | all-reduce | flops 256 | bytes 2048 | tf_op jit(solution)/shard_map/psum | solution.py:67
  452.9 361.2 %all-reduce.4.cloned.1.call-done = (f32[256,256]{1,0:T(8,128)}, f32[256,256]{1,0:T(8,128)}) async-done(((f32[256,256]{1,0:T(8,128)}, f32[256,256]{1,0:T(8,128)}), (f32[256,256]{1,0:T(8,128)}, f32[256,256]{1,0:T(8,128)})) %all-reduce.4.cloned.1.call-update) | async-done | bytes 524304 | tf_op jit(solution)/shard_map/psum | solution.py:67
  814.1 1.7 copy.27
  815.8 1.7 copy.28
  (21 shorter events, 0.2 us)
Async XLA Ops:
  7.2 333.9 %copy-start = (f32[256,256]{1,0:T(8,128)S(1)}, f32[256,256]{1,0:T(8,128)}, u32[]{:S(2)}) copy-start(f32[256,256]{1,0:T(8,128)} %param.16) | copy-start | bytes 786436
  7.2 229.8 %all-gather.2.cloned.1.call-start = ((), (), s32[]{:S(2)}) async-start(), calls=%async_computation.1 | async-start | bytes 12976128 | tf_op jit(solution)/shard_map/all_gather | solution.py:51
  7.9 333.1 %reduce-scatter.2.cloned.1.call-start = ((), (), s32[]{:S(2)}) async-start(), calls=%async_computation.2 | async-start | bytes 417792 | tf_op jit(solution)/shard_map/reduce_scatter | solution.py:61
  236.9 9.0 %copy-start.1 = (bf16[1,1,32,2,128,128]{5,4,3,2,1,0:T(8,128)(2,1)S(1)}, bf16[1,1,32,2,128,128]{5,4,3,2,1,0:T(8,128)(2,1)}, u32[]{:S(2)}) copy-start(bf16[1,1,32,2,128,128]{5,4,3,2,1,0:T(8,128)(2,1)} %param.10) | copy-start | bytes 6291460
  257.6 10.4 %copy-start.4 = (s32[1,1,32,2]{2,3,1,0:T(2,128)S(1)}, s32[1,1,32,2]{2,3,1,0:T(2,128)}, u32[]{:S(2)}) copy-start(s32[1,1,32,2]{2,3,1,0:T(2,128)} %param.12) | copy-start | bytes 772
  268.0 41.5 %copy-start.2 = (f32[256,256]{1,0:T(8,128)S(1)}, f32[256,256]{1,0:T(8,128)}, u32[]{:S(2)}) copy-start(f32[256,256]{1,0:T(8,128)} %param.15) | copy-start | bytes 786436
  268.0 73.0 %copy-start.3 = (f32[24,256]{1,0:T(8,128)S(1)}, f32[24,256]{1,0:T(8,128)}, u32[]{:S(2)}) copy-start(f32[24,256]{1,0:T(8,128)} %param.14) | copy-start | bytes 73732
  268.0 73.0 %copy-start.5 = (f32[256]{0:T(256)S(1)}, f32[256]{0:T(256)}, u32[]{:S(2)}) copy-start(f32[256]{0:T(256)} %param.17) | copy-start | bytes 3076
  275.4 538.7 %all-reduce.4.cloned.1.call-start = ((), (), s32[]{:S(2)}) async-start(), calls=%async_computation.3 | async-start | bytes 1048576 | tf_op jit(solution)/shard_map/psum | solution.py:67
Sparse Core Ops, SparseCore 0:
  11.1 225.7 all-gather.1
  275.5 65.4 reduce-scatter.1
  347.1 466.9 all-reduce.3
where the time goes:
time: 825 us; the launch traced here: 824 us
  waiting for transfers between devices  620 us (75%)
  blocking collectives  138 us (17%)
  local copies, waits for them, and re-layouts  25 us (3%)
  matrix products  24.9 us (3%)
  between operations  15.1 us (2%)
    psum x1, waiting for transfers between devices, on_device(): lax.psum((grad_self, grad_neigh, grad_bias), ('grp', 'mem'))  361 us
    all_gather x1, waiting for transfers between devices, on_device(): piece = lax.all_gather(features, 'mem', axis=0, tiled=True)  227 us
    psum x1, blocking collectives, on_device(): lax.psum((grad_self, grad_neigh, grad_bias), ('grp', 'mem'))  106 us
    unnamed x1, blocking collectives  31.2 us
    reduce_scatter x1, waiting for transfers between devices, on_device(): lax.psum_scatter(summed, 'grp', scatter_dimension=0, tiled=True)  30.5 us
  transfers between devices with their start and end apart: 3, of which 3 were waited for; matrix products, arithmetic and copies ran while one was open for 0% of the time, Pallas kernels for 0%

commit v1 on v0

--- a/solution.py
+++ b/solution.py
@@ -2,6 +2,17 @@
 import jax.numpy as jnp
 from jax import lax
 from jax.sharding import PartitionSpec as P
+from jax.lax import all_to_all, axis_size
+
+slot_wrap = lambda inputs, at_axis: jnp.concatenate(
+    all_to_all(
+        jnp.stack([inputs for _ in range(axis_size("mem"))], 0),
+        concat_axis=0,
+        axis_name="mem",
+        split_axis=0,
+    ),
+    at_axis,
+)
 
 
 def accumulate(masks, place, rows):
@@ -48,7 +59,7 @@
     degree = jnp.einsum(
         "jpt,jpa->ta", place, jnp.sum(masks, axis=3), precision=lax.Precision.HIGHEST
     ).reshape(block)
-    piece = lax.all_gather(features, "mem", axis=0, tiled=True)
+    piece = slot_wrap(features, at_axis=0)
     shards = piece.shape[0] // block
     stacked = piece.reshape(shards * tblocks, tile, width)
     picked = jnp.arange(shards)[:, None] * tblocks + sources

time: 825 us -> 1170 us (1.42)
  waiting for transfers between devices: 620 us -> 939 us
  starting transfers between devices: 0.12 us -> 19 us
    all_to_all x0 -> x1, waiting for transfers between devices: none -> 544 us  [all_to_all(jnp.stack([inputs for _ in range(axis_size('mem'))], 0), conca...]
    all_gather x1 -> x0, waiting for transfers between devices: 227 us -> none  [on_device(): piece = lax.all_gather(features, 'mem', axis=0, tiled=True)]
    all_to_all x0 -> x1, starting transfers between devices: none -> 18.9 us  [all_to_all(jnp.stack([inputs for _ in range(axis_size('mem'))], 0), conca...]
where the time goes in v1:
time: 1170 us
  waiting for transfers between devices  939 us (80%)
  blocking collectives  135 us (12%)
  local copies, waits for them, and re-layouts  31.9 us (3%)
  matrix products  24.8 us (2%)
  starting transfers between devices  19 us (2%)
  between operations  15.4 us (1%)
    all_to_all x1, waiting for transfers between devices, all_to_all(jnp.stack([inputs for _ in range(axis_size('mem'))], 0), conca...  544 us
    psum x1, waiting for transfers between devices, on_device(): lax.psum((grad_self, grad_neigh, grad_bias), ('grp', 'mem'))  361 us
    psum x1, blocking collectives, on_device(): lax.psum((grad_self, grad_neigh, grad_bias), ('grp', 'mem'))  107 us
    reduce_scatter x1, waiting for transfers between devices, on_device(): lax.psum_scatter(summed, 'grp', scatter_dimension=0, tiled=True)  34.7 us
    unnamed x1, blocking collectives  27.9 us
  transfers between devices with their start and end apart: 3, of which 3 were waited for; matrix products, arithmetic and copies ran while one was open for 0% of the time, Pallas kernels for 0%

profile of v1, /device:TPU:1, one launch (start us, length us, event | category | flops | bytes accessed | tf_op | source)
XLA Modules:
  0.0 1165.9 jit_solution(10012685331903534228)
XLA Ops:
  7.2 6.9 stack.2
  14.1 18.9 %all-to-all-start = ((f32[32,384,256]{2,1,0:T(8,128)}), f32[32,384,256]{2,1,0:T(8,128)}, u32[]{:S(2)}, u32[]{:S(2)}) async-start(f32[32,384,256]{2,1,0:T(8,128)} %stack.2), calls=%async_computation | async-start | bytes 25165824 | tf_op jit(solution)/shard_map/all_to_all | solution.py:8
  33.1 0.1 copy.20
  33.2 0.1 reshape.95
  34.0 543.7 %all-to-all-done = f32[32,384,256]{2,1,0:T(8,128)} async-done(((f32[32,384,256]{2,1,0:T(8,128)}), f32[32,384,256]{2,1,0:T(8,128)}, u32[]{:S(2)}, u32[]{:S(2)}) %all-to-all-start) | async-done | bytes 12582944 | tf_op jit(solution)/shard_map/all_to_all | solution.py:8
  577.7 9.0 gather_fusion
  586.7 11.7 %convolution_bitcast_fusion = f32[32,2,128,256]{2,3,1,0:T(8,128)} fusion(f32[32,2,128,256]{3,2,1,0:T(8,128)} %bitcast.35, bf16[1,1,32,2,128,128]{5,4,3,2,1,0:T(8,128)(2,1)S(1)} %copy-done.1), kind=kOutput, calls=%fused_computation.2 | convolution fusion | flops 3221225472 | bytes 18874368 | tf_op jit(solution)/shard_map/jpab,jpbd->jpad/dot_general | solution.py:19
  598.4 10.4 copy.22
  608.8 6.6 convolution_bitcast_fusion.1
  615.3 0.8 copy.23
  616.2 1.3 dynamic-slice
  618.2 0.6 convert_reduce_fusion
  618.8 0.2 convolution_bitcast_fusion.2
  619.0 27.9 %all-reduce = f32[384]{0:T(512)S(1)} all-reduce(f32[384]{0:T(512)S(1)} %convolution_bitcast_fusion.2), channel_id=3, replica_groups=mesh['grp'=16,'mem'=32] {'grp'}, use_global_device_ids=true, to_apply=%region_2.0.clone | all-reduce | flops 384 | bytes 3072
  646.9 0.1 fusion.16
  647.0 1.0 fusion.6
  648.0 34.7 %reduce-scatter.2.cloned.1.call-done = f32[24,256]{1,0:T(8,128)} async-done(((f32[384,256]{1,0:T(8,128)}), f32[24,256]{1,0:T(8,128)}) %reduce-scatter.2.cloned.1.call-update) | async-done | bytes 24592 | tf_op jit(solution)/shard_map/reduce_scatter | solution.py:72
  682.7 1.6 fusion.21
  684.3 1.9 fusion.4
  686.1 1.9 fusion.9
  688.1 106.6 %psum.23 = f32[256]{0:T(256)} all-reduce(f32[256]{0:T(256)S(1)} %get-tuple-element.6), channel_id=1, replica_groups=mesh['grp'=16,'mem'=32] {'grp','mem'}, use_global_device_ids=true, to_apply=%region_6.0 | all-reduce | flops 256 | bytes 2048 | tf_op jit(solution)/shard_map/psum | solution.py:78
  794.7 361.0 %all-reduce.4.cloned.1.call-done = (f32[256,256]{1,0:T(8,128)}, f32[256,256]{1,0:T(8,128)}) async-done(((f32[256,256]{1,0:T(8,128)}, f32[256,256]{1,0:T(8,128)}), (f32[256,256]{1,0:T(8,128)}, f32[256,256]{1,0:T(8,128)})) %all-reduce.4.cloned.1.call-update) | async-done | bytes 524304 | tf_op jit(solution)/shard_map/psum | solution.py:78
  1155.7 1.7 copy.32
  1157.4 1.7 copy.33
  (23 shorter events, 0.2 us)
Async XLA Ops:
  7.2 675.5 %copy-start = (f32[256,256]{1,0:T(8,128)S(1)}, f32[256,256]{1,0:T(8,128)}, u32[]{:S(2)}) copy-start(f32[256,256]{1,0:T(8,128)} %param.16) | copy-start | bytes 786436
  14.1 19.0 %copy-start.6 = (s32[1,1,32,2]{2,3,1,0:T(2,128)S(1)}, s32[1,1,32,2]{2,3,1,0:T(2,128)}, u32[]{:S(2)}) copy-start(s32[1,1,32,2]{2,3,1,0:T(2,128)} %param.11) | copy-start | bytes 772
  14.1 563.6 %all-to-all-start = ((f32[32,384,256]{2,1,0:T(8,128)}), f32[32,384,256]{2,1,0:T(8,128)}, u32[]{:S(2)}, u32[]{:S(2)}) async-start(f32[32,384,256]{2,1,0:T(8,128)} %stack.2), calls=%async_computation | async-start | bytes 25165824 | tf_op jit(solution)/shard_map/all_to_all | solution.py:8
  33.0 649.6 %reduce-scatter.2.cloned.1.call-start = ((), (), s32[]{:S(2)}) async-start(), calls=%async_computation.2 | async-start | bytes 417792 | tf_op jit(solution)/shard_map/reduce_scatter | solution.py:72
  577.7 9.0 copy-start.1
  598.4 10.4 copy-start.4
  608.8 38.2 %copy-start.2 = (f32[256,256]{1,0:T(8,128)S(1)}, f32[256,256]{1,0:T(8,128)}, u32[]{:S(2)}) copy-start(f32[256,256]{1,0:T(8,128)} %param.15) | copy-start | bytes 786436
  608.8 73.9 %copy-start.3 = (f32[24,256]{1,0:T(8,128)S(1)}, f32[24,256]{1,0:T(8,128)}, u32[]{:S(2)}) copy-start(f32[24,256]{1,0:T(8,128)} %param.14) | copy-start | bytes 73732
  608.8 73.9 %copy-start.5 = (f32[256]{0:T(256)S(1)}, f32[256]{0:T(256)}, u32[]{:S(2)}) copy-start(f32[256]{0:T(256)} %param.17) | copy-start | bytes 3076
  616.2 539.6 %all-reduce.4.cloned.1.call-start = ((), (), s32[]{:S(2)}) async-start(), calls=%async_computation.3 | async-start | bytes 1048576 | tf_op jit(solution)/shard_map/psum | solution.py:78
Sparse Core Ops, SparseCore 0:
  616.3 66.2 reduce-scatter.1
  688.7 466.9 all-reduce.3
